TPU v7x, 32 devices: a whole 2x2x4 slice. The times are simulated.
32 devices in a mesh: section: 2 (over y), expert: 16 (over z, x, core).
Axes of the slice: x: 2, y: 2, z: 4, core: 2. Of those that a mesh axis runs over, the one named last changes fastest.
Arguments:
- forward_input: bfloat16 [128, 3584], P('expert', 'section'), may hold values from -6 to 6
- forward_route: int32 [128, 8], P('expert'), may hold values from 0 to 15, all different within a row; in each aligned block of 8 rows (0 to 7, 8 to 15, ...) at most 8 rows name the same one
- forward_weight: float32 [128, 8], P('expert'), may hold values from 0.05 to 0.5
- output_grad: bfloat16 [128, 3584], P('expert', 'section'), may hold values from -6 to 6
- backward_route: int32 [128, 8], P('expert'), may hold values from 0 to 15, all different within a row; in each aligned block of 8 rows (0 to 7, 8 to 15, ...) at most 8 rows name the same one
- backward_weight: float32 [128, 8], P('expert'), may hold values from 0.05 to 0.5
- gate_stash: bfloat16 [16, 128, 2560], P('expert', None, 'section'), may hold values from -6 to 6
- up_stash: bfloat16 [16, 128, 2560], P('expert', None, 'section'), may hold values from -6 to 6
- gate_matrix: bfloat16 [16, 2560, 3584], P('expert', 'section'), may hold values from -0.125 to 0.125
- up_matrix: bfloat16 [16, 2560, 3584], P('expert', 'section'), may hold values from -0.125 to 0.125
- down_matrix: bfloat16 [16, 2560, 3584], P('expert', 'section'), may hold values from -0.15625 to 0.15625
Outputs:
- forward_output: bfloat16 [128, 3584], P('expert', 'section')
- input_grad: bfloat16 [128, 3584], P('expert', 'section')
Inputs may be any that keep to these rules, and one draw needn't show every extreme that they name: `forward_route`: each row names 8 different experts. In each aligned block of 8 rows (the rows of one index of expert) no expert is named by more than 8 rows, a bound that some block reaches. `backward_route`: as for forward_route.
All inputs are finite; a program needn't handle non-finite values.
Results may differ from a plain program's by a relative error of at most 0.0072.
Values may be sent and summed in bfloat16 or wider, within the bound.
No kernel may reach another device: no remote copies, remote signals or barrier semaphores. Data moves between devices by JAX's collectives and lax.ppermute only.
A program may use at most 128 MiB of HBM per device.

v0:
```python
import jax
import jax.numpy as jnp
from jax import lax
from jax.sharding import PartitionSpec as P


def slot_columns(routes, expert_count, capacity):
    chosen = (
        routes[:, :, None] == jnp.arange(expert_count, dtype=jnp.int32)[None, None, :]
    ).astype(jnp.int32)
    per_token = jnp.sum(chosen, axis=1, dtype=jnp.int32)
    earlier = jnp.cumsum(per_token, axis=0, dtype=jnp.int32) - per_token
    position = jnp.sum(chosen * earlier[:, None, :], axis=2, dtype=jnp.int32)
    return routes * capacity + position


def placement_matrix(columns, weights, total_cols):
    matches = (
        columns[:, :, None] == jnp.arange(total_cols, dtype=jnp.int32)[None, None, :]
    ).astype(jnp.float32)
    return jnp.sum(matches * weights[:, :, None], axis=1)


def contract_last(first_operand, second_operand):
    return lax.dot_general(
        first_operand, second_operand, (((1,), (1,)), ((), ())), preferred_element_type=jnp.float32
    )


def contract_first(first_operand, second_operand):
    return lax.dot_general(
        first_operand, second_operand, (((0,), (1,)), ((), ())), preferred_element_type=jnp.float32
    )


def combine_rows(mixing, returned):
    return lax.dot_general(
        mixing,
        returned.astype(jnp.float32),
        (((1,), (1,)), ((), ())),
        precision=lax.Precision.HIGHEST,
        preferred_element_type=jnp.float32,
    )


def shards(
    forward_input,
    forward_route,
    forward_weight,
    output_grad,
    backward_route,
    backward_weight,
    gate_stash,
    up_stash,
    gate_matrix,
    up_matrix,
    down_matrix,
):
    expert_count = lax.axis_size("expert")
    slot_rows = gate_stash.shape[1]
    capacity = slot_rows // expert_count
    feature_cols = forward_input.shape[1]
    gate_weights = gate_matrix[0]
    up_weights = up_matrix[0]
    down_weights = down_matrix[0]
    unit_weight = jnp.ones(forward_weight.shape, jnp.float32)
    forward_cols = slot_columns(forward_route, expert_count, capacity)
    forward_select = placement_matrix(forward_cols, unit_weight, slot_rows)
    forward_mix = placement_matrix(forward_cols, forward_weight, slot_rows)
    backward_cols = slot_columns(backward_route, expert_count, capacity)
    backward_select = placement_matrix(backward_cols, unit_weight, slot_rows)
    backward_mix = placement_matrix(backward_cols, backward_weight, slot_rows)
    select_rows = forward_select.T.astype(jnp.bfloat16)
    sent = jnp.dot(select_rows, forward_input, preferred_element_type=jnp.float32).astype(
        jnp.bfloat16
    )
    arrived = lax.all_to_all(
        sent.reshape(expert_count, capacity, feature_cols),
        "expert",
        split_axis=0,
        concat_axis=0,
        tiled=True,
    )
    arrived = arrived.reshape(slot_rows, feature_cols)
    portion = lax.all_gather(arrived, "section", axis=1, tiled=True)
    gate_part = gate_weights
    up_part = up_weights
    gate_value = contract_last(portion, gate_part)
    up_value = contract_last(portion, up_part)
    hidden = (jax.nn.silu(gate_value) * up_value).astype(jnp.bfloat16)
    down_part = down_weights
    summed = lax.psum_scatter(
        contract_first(down_part, hidden).astype(jnp.bfloat16),
        "section",
        scatter_dimension=0,
        tiled=True,
    )
    expert_output = summed.reshape(feature_cols, expert_count, capacity)
    returned = lax.all_to_all(
        expert_output, "expert", split_axis=1, concat_axis=1, tiled=True
    ).reshape(feature_cols, slot_rows)
    forward_output = combine_rows(forward_mix, returned).astype(jnp.bfloat16)
    sent_grad = jnp.dot(
        backward_mix.T,
        output_grad.astype(jnp.float32),
        precision=lax.Precision.HIGHEST,
        preferred_element_type=jnp.float32,
    ).astype(jnp.bfloat16)
    arrived_grad = lax.all_to_all(
        sent_grad.reshape(expert_count, capacity, feature_cols),
        "expert",
        split_axis=0,
        concat_axis=0,
        tiled=True,
    )
    arrived_grad = arrived_grad.reshape(slot_rows, feature_cols)
    down_part = down_weights
    grad_hidden = contract_last(
        lax.all_gather(arrived_grad, "section", axis=1, tiled=True), down_part
    )
    gate_saved = gate_stash[0].astype(jnp.float32)
    up_saved = up_stash[0].astype(jnp.float32)
    sigmoid_gate = jax.nn.sigmoid(gate_saved)
    grad_gate = (
        grad_hidden * up_saved * sigmoid_gate * (1.0 + gate_saved * (1.0 - sigmoid_gate))
    ).astype(jnp.bfloat16)
    grad_up = (grad_hidden * gate_saved * sigmoid_gate).astype(jnp.bfloat16)
    gate_part = gate_weights
    up_part = up_weights
    summed_grad = lax.psum_scatter(
        (contract_first(gate_part, grad_gate) + contract_first(up_part, grad_up)).astype(
            jnp.bfloat16
        ),
        "section",
        scatter_dimension=0,
        tiled=True,
    )
    expert_grad = summed_grad.reshape(feature_cols, expert_count, capacity)
    returned_grad = lax.all_to_all(
        expert_grad, "expert", split_axis=1, concat_axis=1, tiled=True
    ).reshape(feature_cols, slot_rows)
    input_grad = combine_rows(backward_select, returned_grad).astype(jnp.bfloat16)
    return (forward_output, input_grad)


def solution(mesh):
    in_specs = (
        P("expert", "section"),
        P("expert", None),
        P("expert", None),
        P("expert", "section"),
        P("expert", None),
        P("expert", None),
        P("expert", None, "section"),
        P("expert", None, "section"),
        P("expert", "section", None),
        P("expert", "section", None),
        P("expert", "section", None),
    )
    out_specs = (P("expert", "section"), P("expert", "section"))
    return jax.shard_map(shards, mesh=mesh, in_specs=in_specs, out_specs=out_specs, check_vma=False)
```

profile of v0, /device:TPU:0, one launch (start us, length us, event | category | flops | bytes accessed | tf_op | source)
XLA Modules:
  0.0 145.0 jit_solution(15437782882217925766)
XLA Ops:
  7.2 0.0 copy-start
  7.2 0.0 copy-start.2
  7.2 0.8 convert_reduce_fusion.1
  8.0 1.0 select_reduce_fusion.1
  9.0 0.7 multiply_add_fusion
  9.7 0.8 select_reduce_fusion
  10.5 0.0 copy-done
  10.5 1.3 fusion.33
  11.8 7.4 %all-to-all-start.2 = ((bf16[16,8,1792]{2,1,0:T(8,128)(2,1)}), bf16[16,8,1792]{2,1,0:T(8,128)(2,1)S(1)}, u32[]{:S(2)}, u32[]{:S(2)}) async-start(bf16[16,8,1792]{2,1,0:T(8,128)(2,1)} %fusion.33), calls=%async_computation.3 | async-start | bytes 917504 | tf_op jit(solution)/shard_map/all_to_all | solution.py:109
  19.2 0.8 convert_reduce_fusion.3
  20.0 1.0 select_reduce_fusion.3
  21.0 0.7 multiply_add_fusion.1
  21.7 0.8 convert_reduce_fusion.2
  22.5 1.9 %fusion.34 = bf16[16,8,1792]{2,1,0:T(8,128)(2,1)} fusion(bf16[8,1792]{1,0:T(8,128)(2,1)} %param.11, bf16[8,128]{1,0:T(8,128)(2,1)S(1)} %get-tuple-element.4), kind=kOutput, calls=%fused_computation.22 | convolution fusion | flops 3899392 | bytes 489472 | tf_op jit(solution)/shard_map/dot_general | solution.py:74
  24.3 8.1 %all-to-all-done.2 = bf16[16,8,1792]{2,1,0:T(8,128)(2,1)S(1)} async-done(((bf16[16,8,1792]{2,1,0:T(8,128)(2,1)}), bf16[16,8,1792]{2,1,0:T(8,128)(2,1)S(1)}, u32[]{:S(2)}, u32[]{:S(2)}) %all-to-all-start.2) | async-done | bytes 458784 | tf_op jit(solution)/shard_map/all_to_all | solution.py:109
  32.5 3.9 %all-to-all-start = ((bf16[16,8,1792]{2,1,0:T(8,128)(2,1)}), bf16[16,8,1792]{2,1,0:T(8,128)(2,1)S(1)}, u32[]{:S(2)}, u32[]{:S(2)}) async-start(bf16[16,8,1792]{2,1,0:T(8,128)(2,1)} %fusion.34), calls=%async_computation | async-start | bytes 917504 | tf_op jit(solution)/shard_map/all_to_all | solution.py:77
  36.4 0.0 reduce-scatter.5.cloned.1.call-start
  36.4 0.0 copy-start.1
  36.4 13.7 %all_gather.7 = bf16[128,3584]{1,0:T(8,128)(2,1)S(1)} all-gather(bf16[128,1792]{1,0:T(8,128)(2,1)S(1)} %bitcast.76), channel_id=1, replica_groups=mesh['section'=2,'expert'=16] {'section'}, dimensions={1}, use_global_device_ids=true | all-gather | bytes 1376256 | tf_op jit(solution)/shard_map/all_gather | solution.py:119
  50.1 0.0 slice-start
  50.1 0.0 slice-start.1
  50.1 6.7 %fusion = f32[128,1280]{1,0:T(8,128)S(1)} fusion(bf16[128,3584]{1,0:T(8,128)(2,1)S(1)} %all_gather.7, bf16[1,1280,3584]{2,1,0:T(8,128)(2,1)} %param.21), kind=kOutput, calls=%fused_computation | convolution fusion | flops 1174405120 | bytes 10747904 | tf_op jit(solution)/shard_map/dot_general | solution.py:25
  56.8 0.0 copy-done.2
  56.8 0.0 copy-done.1
  56.8 0.0 slice-start.2
  56.9 0.0 copy-start.3
  56.9 1.4 fusion.4
  58.3 0.0 slice-done
  58.3 0.0 slice-done.1
  58.3 0.0 slice-done.2
  58.3 0.0 copy-done.3
  58.4 2.5 %fusion.24 = bf16[3584,128]{0,1:T(8,128)(2,1)} fusion(f32[128,3584]{1,0:T(8,128)S(1)} %fusion.4, bf16[1,1280,3584]{2,1,0:T(8,128)(2,1)S(1)} %bitcast.75, f32[128,1280]{1,0:T(8,128)S(1)} %fusion, bf16[1,128,1280]{2,1,0:T(8,128)(2,1)S(1)} %copy-done.3, bf16[1,128,1280]{2,1,0:T(8,128)(2,1)S(1)} %copy-done.2), kind=kOutput, calls=%fused_computation.16 | convolution fusion | flops 1177288704 | bytes 13238272 | tf_op jit(solution)/shard_map/dot_general | solution.py:31
  60.8 0.0 reduce-scatter.5.cloned.1.call-update
  60.9 0.0 reduce-scatter.3.cloned.1.call-start
  60.9 0.0 all-to-all-done
  60.9 17.9 %all_gather.6 = bf16[128,3584]{1,0:T(8,128)(2,1)S(1)} all-gather(bf16[128,1792]{1,0:T(8,128)(2,1)S(1)} %bitcast.77), channel_id=1, replica_groups=mesh['section'=2,'expert'=16] {'section'}, dimensions={1}, use_global_device_ids=true | all-gather | bytes 1376256 | tf_op jit(solution)/shard_map/all_gather | solution.py:85
  78.8 6.6 %fusion.10 = f32[128,1280]{1,0:T(8,128)S(1)} fusion(bf16[128,3584]{1,0:T(8,128)(2,1)S(1)} %all_gather.6, bf16[1,1280,3584]{2,1,0:T(8,128)(2,1)} %param.19), kind=kOutput, calls=%fused_computation.10 | convolution fusion | flops 1174405120 | bytes 10747904 | tf_op jit(solution)/shard_map/dot_general | solution.py:25
  85.4 12.3 %fusion.21 = bf16[3584,128]{0,1:T(8,128)(2,1)} fusion(bf16[1,1280,3584]{2,1,0:T(8,128)(2,1)} %param.21, bf16[128,3584]{1,0:T(8,128)(2,1)S(1)} %all_gather.6, bf16[1,1280,3584]{2,1,0:T(8,128)(2,1)} %param.20, f32[128,1280]{1,0:T(8,128)S(1)} %fusion.10), kind=kOutput, calls=%fused_computation.15 | convolution fusion | flops 2350252032 | bytes 20840448 | tf_op jit(solution)/shard_map/dot_general | solution.py:31
  97.7 0.0 reduce-scatter.3.cloned.1.call-update
  97.8 0.0 reduce-scatter.5.cloned.1.call-done
  97.8 5.3 %all-to-all-start.3 = ((bf16[1792,16,8]{0,2,1:T(8,128)(2,1)}), bf16[1792,16,8]{0,2,1:T(8,128)(2,1)S(1)}, u32[]{:S(2)}, u32[]{:S(2)}) async-start(bf16[1792,16,8]{0,2,1:T(8,128)(2,1)} %bitcast.78), calls=%async_computation.5 | async-start | bytes 917504 | tf_op jit(solution)/shard_map/all_to_all | solution.py:139
  103.1 15.3 %reduce-scatter.3.cloned.1.call-done = bf16[1792,128]{0,1:T(8,128)(2,1)} async-done(((bf16[3584,128]{0,1:T(8,128)(2,1)}), bf16[1792,128]{0,1:T(8,128)(2,1)}) %reduce-scatter.3.cloned.1.call-update) | async-done | bytes 458768 | tf_op jit(solution)/shard_map/reduce_scatter | solution.py:92
  118.4 0.0 all-to-all-done.3
  118.4 5.6 %all-to-all-start.1 = ((bf16[1792,16,8]{0,2,1:T(8,128)(2,1)}), bf16[1792,16,8]{0,2,1:T(8,128)(2,1)S(1)}, u32[]{:S(2)}, u32[]{:S(2)}) async-start(bf16[1792,16,8]{0,2,1:T(8,128)(2,1)} %bitcast.79), calls=%async_computation.2 | async-start | bytes 917504 | tf_op jit(solution)/shard_map/all_to_all | solution.py:99
  124.0 0.9 convolution_convert_fusion.2
  124.9 12.3 %all-to-all-done.1 = bf16[1792,16,8]{0,2,1:T(8,128)(2,1)S(1)} async-done(((bf16[1792,16,8]{0,2,1:T(8,128)(2,1)}), bf16[1792,16,8]{0,2,1:T(8,128)(2,1)S(1)}, u32[]{:S(2)}, u32[]{:S(2)}) %all-to-all-start.1) | async-done | bytes 458784 | tf_op jit(solution)/shard_map/all_to_all | solution.py:99
  137.3 0.9 convolution_convert_fusion.3
  (5 shorter events, 0.1 us)
Async XLA Ops:
  7.2 3.3 %copy-start = (bf16[8,1792]{1,0:T(8,128)(2,1)S(1)}, bf16[8,1792]{1,0:T(8,128)(2,1)}, u32[]{:S(2)}) copy-start(bf16[8,1792]{1,0:T(8,128)(2,1)} %param.14) | copy-start | bytes 86020
  7.2 49.6 %copy-start.2 = (bf16[1,128,1280]{2,1,0:T(8,128)(2,1)S(1)}, bf16[1,128,1280]{2,1,0:T(8,128)(2,1)}, u32[]{:S(2)}) copy-start(bf16[1,128,1280]{2,1,0:T(8,128)(2,1)} %param.17) | copy-start | bytes 983044
  11.8 20.6 %all-to-all-start.2 = ((bf16[16,8,1792]{2,1,0:T(8,128)(2,1)}), bf16[16,8,1792]{2,1,0:T(8,128)(2,1)S(1)}, u32[]{:S(2)}, u32[]{:S(2)}) async-start(bf16[16,8,1792]{2,1,0:T(8,128)(2,1)} %fusion.33), calls=%async_computation.3 | async-start | bytes 917504 | tf_op jit(solution)/shard_map/all_to_all | solution.py:109
  32.5 28.5 %all-to-all-start = ((bf16[16,8,1792]{2,1,0:T(8,128)(2,1)}), bf16[16,8,1792]{2,1,0:T(8,128)(2,1)S(1)}, u32[]{:S(2)}, u32[]{:S(2)}) async-start(bf16[16,8,1792]{2,1,0:T(8,128)(2,1)} %fusion.34), calls=%async_computation | async-start | bytes 917504 | tf_op jit(solution)/shard_map/all_to_all | solution.py:77
  36.4 61.4 %reduce-scatter.5.cloned.1.call-start = ((), (), s32[]{:S(2)}) async-start(), calls=%async_computation.7 | async-start | bytes 1376256 | tf_op jit(solution)/shard_map/reduce_scatter | solution.py:130
  36.4 20.4 %copy-start.1 = (bf16[1,1280,3584]{2,1,0:T(8,128)(2,1)S(1)}, bf16[1,1280,3584]{2,1,0:T(8,128)(2,1)}, u32[]{:S(2)}) copy-start(bf16[1,1280,3584]{2,1,0:T(8,128)(2,1)} %param.20) | copy-start | bytes 27525124
  50.1 8.2 %slice-start = ((s8[9175040]{0:T(1024)(128)(4,1)}), s8[4194304]{0:T(1024)(128)(4,1)S(1)}, s32[]{:S(2)}) async-start(s8[9175040]{0:T(1024)(128)(4,1)} %bitcast.74), calls=%async_computation.8 | async-start | bytes 8388608
  50.1 8.2 %slice-start.1 = ((s8[9175040]{0:T(1024)(128)(4,1)}), s8[4194304]{0:T(1024)(128)(4,1)S(1)}, s32[]{:S(2)}) async-start(s8[9175040]{0:T(1024)(128)(4,1)} %bitcast.74), calls=%async_computation.9 | async-start | bytes 8388608
  56.8 1.5 %slice-start.2 = ((s8[9175040]{0:T(1024)(128)(4,1)}), s8[786432]{0:T(1024)(128)(4,1)S(1)}, s32[]{:S(2)}) async-start(s8[9175040]{0:T(1024)(128)(4,1)} %bitcast.74), calls=%async_computation.10 | async-start | bytes 1572864
  56.9 1.5 %copy-start.3 = (bf16[1,128,1280]{2,1,0:T(8,128)(2,1)S(1)}, bf16[1,128,1280]{2,1,0:T(8,128)(2,1)}, u32[]{:S(2)}) copy-start(bf16[1,128,1280]{2,1,0:T(8,128)(2,1)} %param.18) | copy-start | bytes 983044
  60.9 57.5 %reduce-scatter.3.cloned.1.call-start = ((), (), s32[]{:S(2)}) async-start(), calls=%async_computation.6 | async-start | bytes 1376256 | tf_op jit(solution)/shard_map/reduce_scatter | solution.py:92
  97.8 20.6 %all-to-all-start.3 = ((bf16[1792,16,8]{0,2,1:T(8,128)(2,1)}), bf16[1792,16,8]{0,2,1:T(8,128)(2,1)S(1)}, u32[]{:S(2)}, u32[]{:S(2)}) async-start(bf16[1792,16,8]{0,2,1:T(8,128)(2,1)} %bitcast.78), calls=%async_computation.5 | async-start | bytes 917504 | tf_op jit(solution)/shard_map/all_to_all | solution.py:139
  118.4 18.9 %all-to-all-start.1 = ((bf16[1792,16,8]{0,2,1:T(8,128)(2,1)}), bf16[1792,16,8]{0,2,1:T(8,128)(2,1)S(1)}, u32[]{:S(2)}, u32[]{:S(2)}) async-start(bf16[1792,16,8]{0,2,1:T(8,128)(2,1)} %bitcast.79), calls=%async_computation.2 | async-start | bytes 917504 | tf_op jit(solution)/shard_map/all_to_all | solution.py:99
Sparse Core Ops, SparseCore 0:
  61.0 23.5 reduce-scatter.4
  97.9 20.4 reduce-scatter.2
where the time goes:
time: 146 us; the launch traced here: 145 us
  waiting for transfers between devices  35.8 us (25%)
  matrix products  34.6 us (24%)
  blocking collectives  31.5 us (22%)
  starting transfers between devices  22.2 us (15%)
  between operations  14.3 us (10%)
  other arithmetic  6.52 us (4%)
    all_gather x1, blocking collectives, shards(): portion = lax.all_gather(arrived, 'section', axis=1, tiled=True)  17.9 us
    dot_general x3, matrix products, contract_first(): lax.dot_general(first_operand, second_operand, (((0,), (1,)), ((), ())),...  16.2 us
    reduce_scatter x1, waiting for transfers between devices, shards(): lax.psum_scatter(contract_first(down_part, hidden).astype(jnp.bfloat16),...  15.3 us
    all_gather x1, blocking collectives, shards(): lax.all_gather(arrived_grad, 'section', axis=1, tiled=True)  13.7 us
    dot_general x2, matrix products, contract_last(): lax.dot_general(first_operand, second_operand, (((1,), (1,)), ((), ())),...  13.3 us
    all_to_all x1, waiting for transfers between devices, shards(): lax.all_to_all(expert_output, 'expert', split_axis=1, concat_axis=1, tile...  12.3 us
    all_to_all x1, waiting for transfers between devices, shards(): lax.all_to_all(sent_grad.reshape(expert_count, capacity, feature_cols), '...  8.14 us
    all_to_all x1, starting transfers between devices, shards(): lax.all_to_all(sent_grad.reshape(expert_count, capacity, feature_cols), '...  7.36 us
  transfers between devices with their start and end apart: 6, of which 3 were waited for; matrix products, arithmetic and copies ran while one was open for 25% of the time, Pallas kernels for 0%

commit v1 on v0

--- a/solution.py
+++ b/solution.py
@@ -2,6 +2,7 @@
 import jax.numpy as jnp
 from jax import lax
 from jax.sharding import PartitionSpec as P
+from jax.lax import all_to_all, axis_size
 
 
 def slot_columns(routes, expert_count, capacity):
@@ -96,8 +97,11 @@
         tiled=True,
     )
     expert_output = summed.reshape(feature_cols, expert_count, capacity)
-    returned = lax.all_to_all(
-        expert_output, "expert", split_axis=1, concat_axis=1, tiled=True
+    returned = jnp.concatenate(
+        all_to_all(
+            jnp.stack(jnp.split(expert_output, axis_size("expert"), axis=1)), "expert", 0, 0
+        ),
+        axis=1,
     ).reshape(feature_cols, slot_rows)
     forward_output = combine_rows(forward_mix, returned).astype(jnp.bfloat16)
     sent_grad = jnp.dot(

time: 146 us -> 169 us (1.16)
  local copies, waits for them, and re-layouts: 0.04 us -> 21.7 us
  blocking collectives: 31.5 us -> 26.4 us
  matrix products: 34.6 us -> 38.3 us
  waiting for transfers between devices: 35.8 us -> 38.6 us
    unnamed x14 -> x27, local copies, waits for them, and re-layouts: 0.04 us -> 20.4 us
    all_to_all x1, waiting for transfers between devices: 0.01 us -> 12.3 us  [shards(): lax.all_to_all(expert_grad, 'expert', split_axis=1, concat_axis=1, tiled=...]
    reduce_scatter x1, waiting for transfers between devices: 15.3 us -> 5.05 us  [shards(): lax.psum_scatter(contract_first(down_part, hidden).astype(jnp.bfloat16),...]
    all_to_all x1, waiting for transfers between devices: 8.14 us -> 0.01 us  [shards(): lax.all_to_all(sent_grad.reshape(expert_count, capacity, feature_cols), '...]
    all_to_all x1, waiting for transfers between devices: 0.01 us -> 7.89 us  [shards(): lax.all_to_all(sent.reshape(expert_count, capacity, feature_cols), 'exper...]
    all_gather x1, blocking collectives: 17.9 us -> 13.5 us  [shards(): portion = lax.all_gather(arrived, 'section', axis=1, tiled=True)]
    dot_general x3, matrix products: 16.2 us -> 20 us  [contract_first(): lax.dot_general(first_operand, second_operand, (((0,), (1,)), ((), ())),...]
    all_to_all x1, starting transfers between devices: 7.36 us -> 3.89 us  [shards(): lax.all_to_all(sent_grad.reshape(expert_count, capacity, feature_cols), '...]
  transfers between devices with their start and end apart: 6 -> 6, of which waited for: 3 -> 4; matrix products, arithmetic and copies ran while one was open for 25% -> 25% of each run, Pallas kernels for 0% -> 0%
where the time goes in v1:
time: 169 us; the launch traced here: 167 us
  waiting for transfers between devices  38.6 us (23%)
  matrix products  38.3 us (23%)
  blocking collectives  26.4 us (16%)
  local copies, waits for them, and re-layouts  21.7 us (13%)
  starting transfers between devices  20.9 us (12%)
  between operations  14.2 us (8%)
  other arithmetic  6.48 us (4%)
    unnamed x27, local copies, waits for them, and re-layouts  20.4 us
    dot_general x3, matrix products, contract_first(): lax.dot_general(first_operand, second_operand, (((0,), (1,)), ((), ())),...  20 us
    all_gather x1, blocking collectives, shards(): portion = lax.all_gather(arrived, 'section', axis=1, tiled=True)  13.5 us
    dot_general x2, matrix products, contract_last(): lax.dot_general(first_operand, second_operand, (((1,), (1,)), ((), ())),...  13.3 us
    all_to_all x1, waiting for transfers between devices, shards(): all_to_all(jnp.stack(jnp.split(expert_output, axis_size('expert'), axis=1...  13.2 us
    all_gather x1, blocking collectives, shards(): lax.all_gather(arrived_grad, 'section', axis=1, tiled=True)  12.9 us
    all_to_all x1, waiting for transfers between devices, shards(): lax.all_to_all(expert_grad, 'expert', split_axis=1, concat_axis=1, tiled=...  12.3 us
    all_to_all x1, waiting for transfers between devices, shards(): lax.all_to_all(sent.reshape(expert_count, capacity, feature_cols), 'exper...  7.89 us
  transfers between devices with their start and end apart: 6, of which 4 were waited for; matrix products, arithmetic and copies ran while one was open for 25% of the time, Pallas kernels for 0%

profile of v1, /device:TPU:0, one launch (start us, length us, event | category | flops | bytes accessed | tf_op | source)
XLA Modules:
  0.0 166.6 jit_solution(5427254756981021280)
XLA Ops:
  7.2 0.8 convert_reduce_fusion.3
  8.0 1.0 select_reduce_fusion.3
  9.0 0.7 multiply_add_fusion.1
  9.7 0.8 convert_reduce_fusion.2
  10.4 1.1 fusion.34
  11.5 7.4 %all-to-all-start = ((bf16[16,8,1792]{2,1,0:T(8,128)(2,1)}), bf16[16,8,1792]{2,1,0:T(8,128)(2,1)S(1)}, u32[]{:S(2)}, u32[]{:S(2)}) async-start(bf16[16,8,1792]{2,1,0:T(8,128)(2,1)} %fusion.34), calls=%async_computation | async-start | bytes 917504 | tf_op jit(solution)/shard_map/all_to_all | solution.py:78
  18.9 0.8 convert_reduce_fusion.1
  19.7 1.0 select_reduce_fusion.1
  20.7 0.7 multiply_add_fusion
  21.4 0.8 select_reduce_fusion
  22.2 2.1 %fusion.33 = bf16[16,8,1792]{2,1,0:T(8,128)(2,1)} fusion(f32[8,128]{1,0:T(8,128)S(1)} %get-tuple-element.2, bf16[8,1792]{1,0:T(8,128)(2,1)} %param.14), kind=kOutput, calls=%fused_computation.21 | convolution fusion | flops 22249472 | bytes 491520 | tf_op jit(solution)/shard_map/dot_general | solution.py:107
  24.3 7.9 %all-to-all-done = bf16[16,8,1792]{2,1,0:T(8,128)(2,1)S(1)} async-done(((bf16[16,8,1792]{2,1,0:T(8,128)(2,1)}), bf16[16,8,1792]{2,1,0:T(8,128)(2,1)S(1)}, u32[]{:S(2)}, u32[]{:S(2)}) %all-to-all-start) | async-done | bytes 458784 | tf_op jit(solution)/shard_map/all_to_all | solution.py:78
  32.2 3.9 %all-to-all-start.2 = ((bf16[16,8,1792]{2,1,0:T(8,128)(2,1)}), bf16[16,8,1792]{2,1,0:T(8,128)(2,1)S(1)}, u32[]{:S(2)}, u32[]{:S(2)}) async-start(bf16[16,8,1792]{2,1,0:T(8,128)(2,1)} %fusion.33), calls=%async_computation.3 | async-start | bytes 917504 | tf_op jit(solution)/shard_map/all_to_all | solution.py:113
  36.1 0.0 reduce-scatter.3.cloned.1.call-start
  36.1 13.5 %all_gather.6 = bf16[128,3584]{1,0:T(8,128)(2,1)S(1)} all-gather(bf16[128,1792]{1,0:T(8,128)(2,1)S(1)} %bitcast.142), channel_id=1, replica_groups=mesh['section'=2,'expert'=16] {'section'}, dimensions={1}, use_global_device_ids=true | all-gather | bytes 1376256 | tf_op jit(solution)/shard_map/all_gather | solution.py:86
  49.7 12.9 %all_gather.7 = bf16[128,3584]{1,0:T(8,128)(2,1)S(1)} all-gather(bf16[128,1792]{1,0:T(8,128)(2,1)S(1)} %bitcast.143), channel_id=1, replica_groups=mesh['section'=2,'expert'=16] {'section'}, dimensions={1}, use_global_device_ids=true | all-gather | bytes 1376256 | tf_op jit(solution)/shard_map/all_gather | solution.py:123
  62.5 6.6 %fusion.10 = f32[128,1280]{1,0:T(8,128)S(1)} fusion(bf16[128,3584]{1,0:T(8,128)(2,1)S(1)} %all_gather.6, bf16[1,1280,3584]{2,1,0:T(8,128)(2,1)} %param.19), kind=kOutput, calls=%fused_computation.10 | convolution fusion | flops 1174405120 | bytes 10747904 | tf_op jit(solution)/shard_map/dot_general | solution.py:26
  69.1 12.3 %fusion.21 = bf16[3584,128]{0,1:T(8,128)(2,1)} fusion(bf16[1,1280,3584]{2,1,0:T(8,128)(2,1)} %param.21, bf16[128,3584]{1,0:T(8,128)(2,1)S(1)} %all_gather.6, bf16[1,1280,3584]{2,1,0:T(8,128)(2,1)} %param.20, f32[128,1280]{1,0:T(8,128)S(1)} %fusion.10), kind=kOutput, calls=%fused_computation.15 | convolution fusion | flops 2350252032 | bytes 20840448 | tf_op jit(solution)/shard_map/dot_general | solution.py:32
  81.4 0.0 reduce-scatter.3.cloned.1.call-update
  81.5 0.0 reduce-scatter.5.cloned.1.call-start
  81.5 6.7 %fusion = f32[128,1280]{1,0:T(8,128)S(1)} fusion(bf16[128,3584]{1,0:T(8,128)(2,1)S(1)} %all_gather.7, bf16[1,1280,3584]{2,1,0:T(8,128)(2,1)} %param.21), kind=kOutput, calls=%fused_computation | convolution fusion | flops 1174405120 | bytes 10747904 | tf_op jit(solution)/shard_map/dot_general | solution.py:26
  88.3 5.2 %fusion.4 = f32[128,3584]{1,0:T(8,128)S(1)} fusion(bf16[1,1280,3584]{2,1,0:T(8,128)(2,1)} %param.20, f32[128,1280]{1,0:T(8,128)S(1)} %fusion, bf16[1,128,1280]{2,1,0:T(8,128)(2,1)S(1)} %copy-done.1), kind=kOutput, calls=%fused_computation.4 | convolution fusion | flops 1175552000 | bytes 11993088 | tf_op jit(solution)/shard_map/dot_general | solution.py:32
  93.5 2.5 %fusion.24 = bf16[3584,128]{0,1:T(8,128)(2,1)} fusion(f32[128,3584]{1,0:T(8,128)S(1)} %fusion.4, bf16[1,1280,3584]{2,1,0:T(8,128)(2,1)S(1)} %bitcast.141, f32[128,1280]{1,0:T(8,128)S(1)} %fusion, bf16[1,128,1280]{2,1,0:T(8,128)(2,1)S(1)} %copy-done.2, bf16[1,128,1280]{2,1,0:T(8,128)(2,1)S(1)} %copy-done.1), kind=kOutput, calls=%fused_computation.16 | convolution fusion | flops 1177288704 | bytes 13238272 | tf_op jit(solution)/shard_map/dot_general | solution.py:32
  96.0 0.0 reduce-scatter.5.cloned.1.call-update
  96.0 5.0 %reduce-scatter.3.cloned.1.call-done = bf16[1792,128]{0,1:T(8,128)(2,1)} async-done(((bf16[3584,128]{0,1:T(8,128)(2,1)}), bf16[1792,128]{0,1:T(8,128)(2,1)}) %reduce-scatter.3.cloned.1.call-update) | async-done | bytes 458768 | tf_op jit(solution)/shard_map/reduce_scatter | solution.py:93
  101.1 1.3 constant_dynamic-update-slice_fusion.15
  102.4 1.3 constant_dynamic-update-slice_fusion.14
  103.8 1.4 constant_dynamic-update-slice_fusion.13
  105.1 1.4 constant_dynamic-update-slice_fusion.12
  106.5 1.4 constant_dynamic-update-slice_fusion.11
  107.9 1.4 constant_dynamic-update-slice_fusion.10
  109.2 1.4 constant_dynamic-update-slice_fusion.9
  110.6 1.3 constant_dynamic-update-slice_fusion.8
  111.9 1.4 constant_dynamic-update-slice_fusion.7
  113.3 1.4 constant_dynamic-update-slice_fusion.6
  114.6 1.4 constant_dynamic-update-slice_fusion.5
  116.0 1.4 constant_dynamic-update-slice_fusion.4
  117.3 1.4 constant_dynamic-update-slice_fusion.3
  118.7 1.4 constant_dynamic-update-slice_fusion.2
  120.1 1.3 constant_dynamic-update-slice_fusion.1
  121.4 1.3 constant_dynamic-update-slice_fusion
  122.8 5.6 %all-to-all-start.1 = ((bf16[16,1792,1,8]{1,3,2,0:T(8,128)(2,1)}), bf16[16,1792,1,8]{1,3,2,0:T(8,128)(2,1)S(1)}, u32[]{:S(2)}, u32[]{:S(2)}) async-start(bf16[16,1792,1,8]{1,3,2,0:T(8,128)(2,1)} %constant_dynamic-update-slice_fusion), calls=%async_computation.2 | async-start | bytes 917504 | tf_op jit(solution)/shard_map/all_to_all | solution.py:101
  128.4 0.0 reduce-scatter.5.cloned.1.call-done
  128.4 13.2 %all-to-all-done.1 = bf16[16,1792,1,8]{1,3,2,0:T(8,128)(2,1)S(1)} async-done(((bf16[16,1792,1,8]{1,3,2,0:T(8,128)(2,1)}), bf16[16,1792,1,8]{1,3,2,0:T(8,128)(2,1)S(1)}, u32[]{:S(2)}, u32[]{:S(2)}) %all-to-all-start.1) | async-done | bytes 458784 | tf_op jit(solution)/shard_map/all_to_all | solution.py:101
  141.7 3.9 %all-to-all-start.3 = ((bf16[1792,16,8]{0,2,1:T(8,128)(2,1)}), bf16[1792,16,8]{0,2,1:T(8,128)(2,1)S(1)}, u32[]{:S(2)}, u32[]{:S(2)}) async-start(bf16[1792,16,8]{0,2,1:T(8,128)(2,1)} %bitcast.144), calls=%async_computation.5 | async-start | bytes 917504 | tf_op jit(solution)/shard_map/all_to_all | solution.py:143
  145.6 0.9 convolution_convert_fusion.3
  146.5 12.3 %all-to-all-done.3 = bf16[1792,16,8]{0,2,1:T(8,128)(2,1)S(1)} async-done(((bf16[1792,16,8]{0,2,1:T(8,128)(2,1)}), bf16[1792,16,8]{0,2,1:T(8,128)(2,1)S(1)}, u32[]{:S(2)}, u32[]{:S(2)}) %all-to-all-start.3) | async-done | bytes 458784 | tf_op jit(solution)/shard_map/all_to_all | solution.py:143
  158.8 0.9 convolution_convert_fusion.2
  (18 shorter events, 0.1 us)
Async XLA Ops:
  7.2 3.3 %copy-start = (bf16[8,1792]{1,0:T(8,128)(2,1)S(1)}, bf16[8,1792]{1,0:T(8,128)(2,1)}, u32[]{:S(2)}) copy-start(bf16[8,1792]{1,0:T(8,128)(2,1)} %param.11) | copy-start | bytes 86020
  11.5 20.6 %all-to-all-start = ((bf16[16,8,1792]{2,1,0:T(8,128)(2,1)}), bf16[16,8,1792]{2,1,0:T(8,128)(2,1)S(1)}, u32[]{:S(2)}, u32[]{:S(2)}) async-start(bf16[16,8,1792]{2,1,0:T(8,128)(2,1)} %fusion.34), calls=%async_computation | async-start | bytes 917504 | tf_op jit(solution)/shard_map/all_to_all | solution.py:78
  32.2 17.5 %all-to-all-start.2 = ((bf16[16,8,1792]{2,1,0:T(8,128)(2,1)}), bf16[16,8,1792]{2,1,0:T(8,128)(2,1)S(1)}, u32[]{:S(2)}, u32[]{:S(2)}) async-start(bf16[16,8,1792]{2,1,0:T(8,128)(2,1)} %fusion.33), calls=%async_computation.3 | async-start | bytes 917504 | tf_op jit(solution)/shard_map/all_to_all | solution.py:113
  36.1 65.0 %reduce-scatter.3.cloned.1.call-start = ((), (), s32[]{:S(2)}) async-start(), calls=%async_computation.6 | async-start | bytes 1376256 | tf_op jit(solution)/shard_map/reduce_scatter | solution.py:93
  81.4 6.8 %copy-start.1 = (bf16[1,128,1280]{2,1,0:T(8,128)(2,1)S(1)}, bf16[1,128,1280]{2,1,0:T(8,128)(2,1)}, u32[]{:S(2)}) copy-start(bf16[1,128,1280]{2,1,0:T(8,128)(2,1)} %param.17) | copy-start | bytes 983044
  81.5 47.0 %reduce-scatter.5.cloned.1.call-start = ((), (), s32[]{:S(2)}) async-start(), calls=%async_computation.7 | async-start | bytes 1376256 | tf_op jit(solution)/shard_map/reduce_scatter | solution.py:134
  81.5 12.0 %slice-start = ((s8[9175040]{0:T(1024)(128)(4,1)}), s8[4194304]{0:T(1024)(128)(4,1)S(1)}, s32[]{:S(2)}) async-start(s8[9175040]{0:T(1024)(128)(4,1)} %bitcast.140), calls=%async_computation.8 | async-start | bytes 8388608
  81.5 12.0 %slice-start.1 = ((s8[9175040]{0:T(1024)(128)(4,1)}), s8[786432]{0:T(1024)(128)(4,1)S(1)}, s32[]{:S(2)}) async-start(s8[9175040]{0:T(1024)(128)(4,1)} %bitcast.140), calls=%async_computation.9 | async-start | bytes 1572864
  88.3 5.2 %slice-start.2 = ((s8[9175040]{0:T(1024)(128)(4,1)}), s8[4194304]{0:T(1024)(128)(4,1)S(1)}, s32[]{:S(2)}) async-start(s8[9175040]{0:T(1024)(128)(4,1)} %bitcast.140), calls=%async_computation.10 | async-start | bytes 8388608
  88.3 5.2 %copy-start.2 = (bf16[1,128,1280]{2,1,0:T(8,128)(2,1)S(1)}, bf16[1,128,1280]{2,1,0:T(8,128)(2,1)}, u32[]{:S(2)}) copy-start(bf16[1,128,1280]{2,1,0:T(8,128)(2,1)} %param.18) | copy-start | bytes 983044
  122.8 18.9 %all-to-all-start.1 = ((bf16[16,1792,1,8]{1,3,2,0:T(8,128)(2,1)}), bf16[16,1792,1,8]{1,3,2,0:T(8,128)(2,1)S(1)}, u32[]{:S(2)}, u32[]{:S(2)}) async-start(bf16[16,1792,1,8]{1,3,2,0:T(8,128)(2,1)} %constant_dynamic-update-slice_fusion), calls=%async_computation.2 | async-start | bytes 917504 | tf_op jit(solution)/shard_map/all_to_all | solution.py:101
  141.7 17.2 %all-to-all-start.3 = ((bf16[1792,16,8]{0,2,1:T(8,128)(2,1)}), bf16[1792,16,8]{0,2,1:T(8,128)(2,1)S(1)}, u32[]{:S(2)}, u32[]{:S(2)}) async-start(bf16[1792,16,8]{0,2,1:T(8,128)(2,1)} %bitcast.144), calls=%async_computation.5 | async-start | bytes 917504 | tf_op jit(solution)/shard_map/all_to_all | solution.py:143
Sparse Core Ops, SparseCore 0:
  81.6 19.4 reduce-scatter.2
  103.4 18.8 reduce-scatter.4
